TPU v7x, 128 devices: a whole 4x4x4 slice. The times are simulated.
128 devices in a mesh: leaf: 4 (over y), row: 8 (over z, core), col: 4 (over x).
Axes of the slice: x: 4, y: 4, z: 4, core: 2. Of those that a mesh axis runs over, the one named last changes fastest.
Arguments:
- sigma_top: float32 [1024, 1024], P(('leaf', 'row'), 'col')
- panels: float32 [4, 7, 1024, 512], P('leaf', None, 'row', 'col'), may hold values from -0.1875 to 0.1875
- inverse_diag: float32 [4, 7, 512, 512], P('leaf', None, 'col')
- slot_lists: int32 [4, 6, 8], P('leaf'), may hold values from -1 to 11, as said below
- parent_links: int32 [4, 4], P('leaf'), may hold values from 1 to 2
Outputs:
- ancestor_block: float32 [4, 7, 1024, 512], P('leaf', None, 'row', 'col')
- diagonal_block: float32 [4, 7, 512, 512], P('leaf', None, None, 'col')
Inputs may be any that keep to these rules, and one draw needn't show every extreme that they name: `slot_lists`: in every row, entries 0 to 3 are 8 to 11 in order (the parent's own tiles); then come 1 to 3 distinct parent ancestor slots, below 8 for supernodes 1 and 2 and below 4 for supernodes 3 to 6; the rest are -1, so every row has padding. `parent_links`: each supernode 3 to 6 has supernode 1 or 2 as its parent. `sigma_top`: symmetric.
All inputs are finite; a program needn't handle non-finite values.
Results may differ from a plain program's by a relative error of at most 0.0001.
Values sent between devices are 32-bit elements; how exact they have to be, the bound alone decides.
A program may use at most 128 MiB of HBM per device.

v0:
```python
import jax
import jax.numpy as jnp
from jax import lax
from jax.sharding import PartitionSpec as P

TILE = 128
HIGHEST = lax.Precision.HIGHEST


def mm(a, b):
    return jnp.matmul(a, b, precision=HIGHEST, preferred_element_type=jnp.float32)


def tile_rows(matrix, index, tile):
    return lax.dynamic_slice_in_dim(matrix, index * tile, tile, 0)


def tile_cols(matrix, index, tile):
    return lax.dynamic_slice_in_dim(matrix, index * tile, tile, 1)


def scatter_factor(factor_col, slots, positions, tile):
    tiles = factor_col.reshape(slots.shape[0], tile, factor_col.shape[1])
    hits = slots[:, None] == jnp.arange(positions, dtype=slots.dtype)[None, :]
    present = jnp.any(hits, axis=0)
    source = jnp.argmax(hits, axis=0)
    moved = jnp.take(tiles, source, axis=0)
    moved = jnp.where(present[:, None, None], moved, 0.0)
    return moved.reshape(positions * tile, factor_col.shape[1])


def pick_transposed(column_block, picks, tile):
    tiles = column_block.reshape(-1, tile, tile)
    chosen = jnp.take(tiles, jnp.maximum(picks, 0), axis=0)
    chosen = jnp.where((picks >= 0)[:, None, None], chosen, 0.0)
    return jnp.transpose(chosen, (2, 0, 1)).reshape(tile, picks.shape[0] * tile)


def body(sigma_top, panels, inverse_diag, slot_lists, parent_links):
    tile = TILE
    row_count = lax.axis_size("row")
    col_count = lax.axis_size("col")
    leaf_count = lax.axis_size("leaf")
    r = lax.axis_index("row")
    c = lax.axis_index("col")
    panel = panels[0]
    inverse = inverse_diag[0]
    picks_all = slot_lists[0]
    parents = parent_links[0]
    nodes = panel.shape[0]
    width = inverse.shape[2]
    own_tiles = width // tile
    slot_count = picks_all.shape[1]
    positions = slot_count + own_tiles
    band = width // row_count
    partial_factor = mm(panel, inverse)
    factor_rows = lax.psum(partial_factor, "col")
    living = jnp.concatenate([jnp.ones((1, slot_count), jnp.bool_), picks_all >= 0], axis=0)
    live_here = jnp.take(living, r, axis=1).astype(jnp.float32)
    factor_rows = factor_rows * live_here[:, None, None]
    factor_tile = lax.dynamic_slice_in_dim(factor_rows, c * tile, tile, 2)
    factor_cols = lax.all_gather(factor_tile, "row", axis=1, tiled=True)
    inverse_band = lax.dynamic_slice_in_dim(inverse, r * band, band, 2)
    partial_gram = mm(jnp.transpose(inverse_band, (0, 2, 1)), inverse)
    gram_piece = lax.psum_scatter(partial_gram, "col", scatter_dimension=2, tiled=True)
    local_rows, local_cols = sigma_top.shape
    gathered = lax.all_gather(sigma_top, ("leaf", "row", "col"), axis=0)
    sigma = gathered.reshape(leaf_count * row_count, col_count, local_rows, local_cols)
    sigma = jnp.transpose(sigma, (0, 2, 1, 3)).reshape(
        leaf_count * row_count * local_rows, col_count * local_cols
    )

    def diag_partial(first, products):
        rows = factor_rows[first : first + products.shape[0]]
        return mm(jnp.transpose(rows, (0, 2, 1)), products)

    def reduce_and_gather(first, products):
        count = products.shape[0]
        piece = lax.psum_scatter(
            diag_partial(first, products), "row", scatter_dimension=1, tiled=True
        )
        piece = piece + gram_piece[first : first + count]
        both = jnp.concatenate([products, piece], axis=1)
        everything = lax.all_gather(both, ("row", "col"), axis=0)
        everything = everything.reshape(row_count, col_count, count, tile + band, tile)
        product_full = jnp.transpose(everything[:, :, :, :tile], (2, 0, 3, 1, 4)).reshape(
            count, row_count * tile, col_count * tile
        )
        diag_full = jnp.transpose(everything[:, :, :, tile:], (2, 0, 3, 1, 4)).reshape(
            count, row_count * band, col_count * tile
        )
        return (product_full, diag_full)

    own_row = jnp.minimum(r, own_tiles - 1)
    upper = r < own_tiles
    product_0 = mm(tile_rows(sigma, r, tile), factor_cols[0])
    product_full_0, diag_full_0 = reduce_and_gather(0, product_0[None])
    product_full_0 = product_full_0[0]
    diag_full_0 = diag_full_0[0]
    level_1 = []
    for node in (1, 2):
        slots = picks_all[node - 1]
        spread = scatter_factor(factor_cols[node], slots, positions, tile)
        top_row = jnp.concatenate(
            [
                -jnp.transpose(tile_cols(product_full_0, own_row, tile)),
                tile_rows(diag_full_0, own_row, tile),
            ],
            axis=1,
        )
        source = slots[jnp.maximum(r, own_tiles)]
        source_row = jnp.maximum(source, 0)
        low_row = jnp.concatenate(
            [tile_rows(sigma, source_row, tile), -tile_rows(product_full_0, source_row, tile)],
            axis=1,
        )
        low_row = jnp.where(source >= 0, low_row, 0.0)
        row = jnp.where(upper, top_row, low_row)
        level_1.append(mm(row, spread))
    product_1 = jnp.stack(level_1)
    product_full_1, diag_full_1 = reduce_and_gather(1, product_1)
    level_2 = []
    for node in range(3, nodes):
        slots = picks_all[node - 1]
        parent = parents[node - 3] - 1
        parent_slots = jnp.take(picks_all, parent, axis=0)
        product_p = jnp.take(product_full_1, parent, axis=0)
        diag_p = jnp.take(diag_full_1, parent, axis=0)
        spread = scatter_factor(factor_cols[node], slots, positions, tile)
        top_row = jnp.concatenate(
            [-jnp.transpose(tile_cols(product_p, own_row, tile)), tile_rows(diag_p, own_row, tile)],
            axis=1,
        )
        source = slots[jnp.maximum(r, own_tiles)]
        source_row = jnp.clip(source, 0, own_tiles - 1)
        corner = pick_transposed(
            -tile_cols(product_full_0, source_row, tile), parent_slots[own_tiles:], tile
        )
        low_row = jnp.concatenate(
            [
                tile_rows(diag_full_0, source_row, tile),
                corner,
                -tile_rows(product_p, source_row, tile),
            ],
            axis=1,
        )
        low_row = jnp.where(source >= 0, low_row, 0.0)
        row = jnp.where(upper, top_row, low_row)
        level_2.append(mm(row, spread))
    product_2 = jnp.stack(level_2)
    first_2 = 3
    count_2 = product_2.shape[0]
    gram_rows = jnp.zeros((count_2, width, tile), jnp.float32)
    gram_rows = lax.dynamic_update_slice_in_dim(
        gram_rows, gram_piece[first_2 : first_2 + count_2], r * band, 1
    )
    diag_2 = lax.psum(diag_partial(first_2, product_2) + gram_rows, "row")
    products = jnp.concatenate([product_0[None], product_1, product_2], axis=0)
    diag_cols = jnp.concatenate(
        [
            tile_cols(diag_full_0, c, tile)[None],
            lax.dynamic_slice_in_dim(diag_full_1, c * tile, tile, 2),
            diag_2,
        ],
        axis=0,
    )
    return ((-products)[None], diag_cols[None])


def solution(mesh):
    return jax.shard_map(
        body,
        mesh=mesh,
        in_specs=(
            P(("leaf", "row"), "col"),
            P("leaf", None, "row", "col"),
            P("leaf", None, "col", None),
            P("leaf", None, None),
            P("leaf", None),
        ),
        out_specs=(P("leaf", None, "row", "col"), P("leaf", None, None, "col")),
        check_vma=False,
    )
```

profile of v0, /device:TPU:0, one launch (start us, length us, event | category | flops | bytes accessed | tf_op | source)
XLA Modules:
  0.0 459.2 jit_solution(14943117877159287603)
XLA Ops:
  9.5 3.9 fusion.2
  14.3 57.6 %all-reduce.4.cloned.1.call-done = f32[7,128,512]{2,1,0:T(8,128)} async-done(((f32[7,128,512]{2,1,0:T(8,128)}), f32[7,128,512]{2,1,0:T(8,128)}) %all-reduce.4.cloned.1.call-update) | async-done | bytes 1835024 | tf_op jit(solution)/shard_map/psum | solution.py:57
  72.0 1.8 broadcast_multiply_fusion
  75.9 2.3 fusion
  78.3 18.1 %all-gather.10.cloned.1.call-done = f32[4096,256]{1,0:T(8,128)} async-done(((f32[32,256]{1,0:T(8,128)}), f32[4096,256]{1,0:T(8,128)}) %all-gather.10.cloned.1.call-update) | async-done | bytes 4194320 | tf_op jit(solution)/shard_map/all_gather | solution.py:67
  96.3 5.8 %copy.83 = f32[32,4,32,256]{3,1,2,0:T(4,128)S(1)} copy(f32[32,4,32,256]{3,2,1,0:T(8,128)} %bitcast.194) | data formatting | bytes 8388608 | tf_op jit(solution)/shard_map/reshape | solution.py:68
  102.2 3.0 copy.124
  105.1 20.2 %all-gather.8.cloned.1.call-done = f32[7,1024,128]{2,1,0:T(8,128)} async-done(((f32[7,128,128]{2,1,0:T(8,128)}), f32[7,1024,128]{2,1,0:T(8,128)}) %all-gather.8.cloned.1.call-update) | async-done | bytes 3670032 | tf_op jit(solution)/shard_map/all_gather | solution.py:62
  125.3 2.5 bitcast_dynamic-update-slice_fusion.6
  129.2 30.5 %reduce-scatter.4.cloned.1.call-done = f32[1,64,128]{2,1,0:T(8,128)} async-done(((f32[1,512,128]{2,1,0:T(8,128)}), f32[1,64,128]{2,1,0:T(8,128)}) %reduce-scatter.4.cloned.1.call-update) | async-done | bytes 32784 | tf_op jit(solution)/shard_map/reduce_scatter | solution.py:79
  170.4 3.1 fusion.102
  176.4 2.3 select_select_fusion.4
  179.7 2.3 constant_dynamic-slice_fusion.22
  182.0 23.9 %all-gather.12.cloned.1.call-done = f32[32,192,128]{2,1,0:T(8,128)} async-done(((f32[1,192,128]{2,1,0:T(8,128)}), f32[32,192,128]{2,1,0:T(8,128)}) %all-gather.12.cloned.1.call-update) | async-done | bytes 3145744 | tf_op jit(solution)/shard_map/all_gather | solution.py:84
  207.3 3.2 slice.189
  210.5 2.9 copy.114
  213.3 2.1 copy.133
  219.5 1.8 copy.117
  221.3 1.7 neg.74
  224.9 2.9 bitcast_dynamic-update-slice_fusion.5
  227.8 1.6 bitcast_dynamic-update-slice_fusion.4
  229.4 1.8 fusion.71
  231.2 30.5 %reduce-scatter.8.cloned.1.call-done = f32[2,64,128]{2,1,0:T(8,128)} async-done(((f32[2,512,128]{2,1,0:T(8,128)}), f32[2,64,128]{2,1,0:T(8,128)}) %reduce-scatter.8.cloned.1.call-update) | async-done | bytes 65552 | tf_op jit(solution)/shard_map/reduce_scatter | solution.py:79
  274.2 2.5 gather_fusion.7
  280.4 2.3 select_select_fusion.1
  285.9 1.9 copy.123
  287.8 2.1 copy.108
  290.8 1.7 gather_fusion.6
  299.2 12.6 %all-gather.14.cloned.1.call-done = f32[64,192,128]{2,1,0:T(8,128)} async-done(((f32[2,192,128]{2,1,0:T(8,128)}), f32[64,192,128]{2,1,0:T(8,128)}) %all-gather.14.cloned.1.call-update) | async-done | bytes 6291472 | tf_op jit(solution)/shard_map/all_gather | solution.py:84
  311.9 3.2 slice.195
  315.0 4.7 %slice.194 = f32[8,4,2,128,128]{4,3,2,1,0:T(8,128)} slice(f32[8,4,2,192,128]{4,3,2,1,0:T(8,128)} %bitcast.193), slice={[0:8], [0:4], [0:2], [0:128], [0:128]} | slice | bytes 8388608 | tf_op jit(solution)/shard_map/slice | solution.py:86
  319.8 5.3 %copy.118 = f32[8,4,2,128,128]{3,0,4,1,2:T(8,128)} copy(f32[8,4,2,128,128]{4,3,2,1,0:T(8,128)} %slice.194) | data formatting | bytes 8388608
  325.0 4.9 %reshape.293 = f32[2,1024,512]{1,2,0:T(8,128)} reshape(f32[2,8,128,4,128]{2,1,4,3,0:T(8,128)} %bitcast.183) | data formatting | bytes 8388608 | tf_op jit(solution)/shard_map/reshape | solution.py:86
  329.9 4.3 copy.134
  334.2 3.1 reshape.294
  337.3 4.2 select_bitcast_fusion.4
  345.8 7.9 %select_bitcast_fusion = (f32[1024,512]{0,1:T(8,128)}, f32[1,1024,512]{1,2,0:T(8,128)}, f32[1,1024,512]{1,2,0:T(8,128)}, f32[1,1024,512]{1,2,0:T(8,128)}) fusion(f32[2,1024,512]{1,2,0:T(8,128)} %reshape.293, s32[]{:T(128)S(6)} %select_n.346, pred[]{:T(512)S(6)} %and.78, s32[]{:T(128)S(6)} %select_n.326, s32[]{:T(128)S(6)} %select_n.316, s32[]{:T(128)S(6)} %select_n.336), kind=kLoop, calls=%fused_computation.12 | loop fusion | flops 524288 | bytes 16777232 | tf_op jit(solution)/shard_map/jit(_take)/select_n | solution.py:127
  353.6 2.9 copy.121
  356.6 1.9 select_bitcast_fusion.2
  360.5 1.9 negate_bitcast_fusion
  363.7 3.0 copy.119
  366.7 1.9 select_bitcast_fusion.3
  370.6 2.9 copy.122
  373.5 1.9 select_bitcast_fusion.1
  377.5 3.3 bitcast_dynamic-update-slice_fusion.3
  385.6 1.8 fusion.62
  391.4 57.6 %all-reduce.6.cloned.1.call-done = f32[4,512,128]{2,1,0:T(8,128)} async-done(((f32[4,512,128]{2,1,0:T(8,128)}), f32[4,512,128]{2,1,0:T(8,128)}) %all-reduce.6.cloned.1.call-update) | async-done | bytes 1048592 | tf_op jit(solution)/shard_map/psum | solution.py:157
  449.1 2.6 maximum_bitcast_fusion
  (201 shorter events, 65.0 us)
Async XLA Ops:
  8.0 1.5 copy-start
  8.0 6.0 %copy-start.37 = (s32[1,6,8]{2,0,1:T(1,128)S(1)}, s32[1,6,8]{2,0,1:T(1,128)}, u32[]{:S(2)}) copy-start(s32[1,6,8]{2,0,1:T(1,128)} %param.18) | copy-start | bytes 580
  8.0 63.9 %all-reduce.4.cloned.1.call-start = ((), (), s32[]{:S(2)}) async-start(), calls=%async_computation.3 | async-start | bytes 3670016 | tf_op jit(solution)/shard_map/psum | solution.py:57
  13.4 82.9 %all-gather.10.cloned.1.call-start = ((), (), s32[]{:S(2)}) async-start(), calls=%async_computation.9 | async-start | bytes 4227072 | tf_op jit(solution)/shard_map/all_gather | solution.py:67
  14.0 111.3 %all-gather.8.cloned.1.call-start = ((), (), s32[]{:S(2)}) async-start(), calls=%async_computation.4 | async-start | bytes 4128768 | tf_op jit(solution)/shard_map/all_gather | solution.py:62
  73.7 1.2 copy-start.2
  75.8 53.4 %reduce-scatter.6.cloned.1.call-start = ((), (), s32[]{:S(2)}) async-start(), calls=%async_computation.6 | async-start | bytes 1146880 | tf_op jit(solution)/shard_map/reduce_scatter | solution.py:65
  78.2 81.5 %reduce-scatter.4.cloned.1.call-start = ((), (), s32[]{:S(2)}) async-start(), calls=%async_computation.5 | async-start | bytes 294912 | tf_op jit(solution)/shard_map/reduce_scatter | solution.py:79
  102.1 25.6 %copy-start.3 = (f32[7,128,512]{2,1,0:T(8,128)S(1)}, f32[7,128,512]{2,1,0:T(8,128)}, u32[]{:S(2)}) copy-start(f32[7,128,512]{2,1,0:T(8,128)} %copy-done.2) | copy-start | bytes 5505028
  129.1 76.9 %all-gather.12.cloned.1.call-start = ((), (), s32[]{:S(2)}) async-start(), calls=%async_computation.10 | async-start | bytes 3244032 | tf_op jit(solution)/shard_map/all_gather | solution.py:84
  161.2 100.5 %reduce-scatter.8.cloned.1.call-start = ((), (), s32[]{:S(2)}) async-start(), calls=%async_computation.7 | async-start | bytes 589824 | tf_op jit(solution)/shard_map/reduce_scatter | solution.py:79
  176.4 2.3 copy-start.12
  216.2 2.3 copy-start.5
  223.8 4.0 copy-start.16
  223.8 4.0 copy-start.21
  223.8 4.0 copy-start.30
  229.4 34.2 %copy-start.38 = (s32[1,4]{1,0:T(1,128)S(1)}, s32[1,4]{1,0:T(1,128)}, u32[]{:S(2)}) copy-start(s32[1,4]{1,0:T(1,128)} %param.19) | copy-start | bytes 52
  229.4 47.4 %copy-start.7 = (f32[1,1024,128]{2,1,0:T(8,128)S(1)}, f32[1,1024,128]{2,1,0:T(8,128)}, u32[]{:S(2)}) copy-start(f32[1,1024,128]{2,1,0:T(8,128)} %get-tuple-element.69) | copy-start | bytes 1572868
  231.2 47.1 %copy-start.6 = (f32[1,1024,128]{2,1,0:T(8,128)S(1)}, f32[1,1024,128]{2,1,0:T(8,128)}, u32[]{:S(2)}) copy-start(f32[1,1024,128]{2,1,0:T(8,128)} %get-tuple-element.71) | copy-start | bytes 1572868
  231.2 80.7 %all-gather.14.cloned.1.call-start = ((), (), s32[]{:S(2)}) async-start(), calls=%async_computation.11 | async-start | bytes 6488064 | tf_op jit(solution)/shard_map/all_gather | solution.py:84
  263.3 185.8 %all-reduce.6.cloned.1.call-start = ((), (), s32[]{:S(2)}) async-start(), calls=%async_computation.8 | async-start | bytes 2097152 | tf_op jit(solution)/shard_map/psum | solution.py:157
  280.4 2.3 copy-start.11
  280.4 3.4 copy-start.10
  283.8 6.0 %copy-start.19 = (f32[1024,128]{0,1:T(8,128)S(1)}, f32[1024,128]{0,1:T(8,128)}, u32[]{:S(2)}) copy-start(f32[1024,128]{0,1:T(8,128)} %get-tuple-element.76) | copy-start | bytes 1572868
  285.9 7.6 %copy-start.18 = (f32[1024,128]{0,1:T(8,128)S(1)}, f32[1024,128]{0,1:T(8,128)}, u32[]{:S(2)}) copy-start(f32[1024,128]{0,1:T(8,128)} %get-tuple-element.77) | copy-start | bytes 1572868
  290.8 6.0 %copy-start.17 = (f32[1024,128]{0,1:T(8,128)S(1)}, f32[1024,128]{0,1:T(8,128)}, u32[]{:S(2)}) copy-start(f32[1024,128]{0,1:T(8,128)} %get-tuple-element.78) | copy-start | bytes 1572868
  293.7 4.9 %copy-start.22 = (f32[1024,128]{1,0:T(8,128)S(1)}, f32[1024,128]{1,0:T(8,128)}, u32[]{:S(2)}) copy-start(f32[1024,128]{1,0:T(8,128)} %copy.108) | copy-start | bytes 1572868
  356.6 2.7 copy-start.34
  359.3 4.1 copy-start.31
  366.7 2.7 copy-start.33
  373.5 2.7 copy-start.32
  377.4 3.4 copy-start.8
  377.4 3.4 copy-start.15
  377.4 3.4 copy-start.24
  377.4 3.4 copy-start.26
  377.4 3.4 copy-start.29
  377.4 5.0 %copy-start.9 = (f32[128,1536]{1,0:T(8,128)S(1)}, f32[128,1536]{1,0:T(8,128)}, u32[]{:S(2)}) copy-start(f32[128,1536]{1,0:T(8,128)} %copy.106) | copy-start | bytes 2359300
  377.4 5.0 %copy-start.14 = (f32[12,128,128]{2,1,0:T(8,128)S(1)}, f32[12,128,128]{2,1,0:T(8,128)}, u32[]{:S(2)}) copy-start(f32[12,128,128]{2,1,0:T(8,128)} %select_select_fusion.1) | copy-start | bytes 2359300
  377.4 5.0 %copy-start.23 = (f32[128,512]{1,0:T(8,128)S(1)}, f32[128,512]{1,0:T(8,128)}, u32[]{:S(2)}) copy-start(f32[128,512]{1,0:T(8,128)} %get-tuple-element.87) | copy-start | bytes 786436
  377.4 5.0 %copy-start.27 = (f32[128,512]{1,0:T(8,128)S(1)}, f32[128,512]{1,0:T(8,128)}, u32[]{:S(2)}) copy-start(f32[128,512]{1,0:T(8,128)} %dynamic-slice_negate_fusion.5) | copy-start | bytes 786436
  377.4 5.0 %copy-start.28 = (f32[128,512]{1,0:T(8,128)S(1)}, f32[128,512]{1,0:T(8,128)}, u32[]{:S(2)}) copy-start(f32[128,512]{1,0:T(8,128)} %copy.105) | copy-start | bytes 786436
  380.8 3.2 copy-start.13
  380.8 3.2 copy-start.20
  380.8 3.2 copy-start.25
  385.6 1.8 copy-start.36
  387.4 2.0 copy-start.35
  387.4 1.0 copy-start.4
  390.2 61.4 %copy-start.1 = (f32[1,7,128,512]{3,2,1,0:T(8,128)S(1)}, f32[1,7,128,512]{3,2,1,0:T(8,128)}, u32[]{:S(2)}) copy-start(f32[1,7,128,512]{3,2,1,0:T(8,128)} %param.17) | copy-start | bytes 5505028
Sparse Core Ops, SparseCore 0:
  13.5 58.3 all-reduce.3
  79.1 22.6 reduce-scatter.5
  129.2 30.4 reduce-scatter.3
  162.1 43.8 all-gather.11
  231.3 30.3 reduce-scatter.7
  263.8 48.0 all-gather.13
Sparse Core Ops, SparseCore 1:
  17.0 79.3 all-gather.9
  98.5 26.8 all-gather.7
  388.5 60.5 all-reduce.5
where the time goes:
time: 461 us; the launch traced here: 459 us
  waiting for transfers between devices  252 us (55%)
  local copies, waits for them, and re-layouts  100 us (22%)
  other arithmetic  53.9 us (12%)
  between operations  26.5 us (6%)
  matrix products  26 us (6%)
    reduce_scatter x2, waiting for transfers between devices, reduce_and_gather(): lax.psum_scatter(diag_partial(first, products), 'row', scatter_dimension=...  61 us
    psum x1, waiting for transfers between devices, body(): factor_rows = lax.psum(partial_factor, 'col')  57.6 us
    psum x1, waiting for transfers between devices, body(): diag_2 = lax.psum(diag_partial(first_2, product_2) + gram_rows, 'row')  57.6 us
    all_gather x2, waiting for transfers between devices, reduce_and_gather(): everything = lax.all_gather(both, ('row', 'col'), axis=0)  36.5 us
    unnamed x92, local copies, waits for them, and re-layouts  35.4 us
    dot_general x12, matrix products, mm(): jnp.matmul(a, b, precision=HIGHEST, preferred_element_type=jnp.float32)  26 us
    all_gather x1, waiting for transfers between devices, body(): factor_cols = lax.all_gather(factor_tile, 'row', axis=1, tiled=True)  20.2 us
    all_gather x1, waiting for transfers between devices, body(): gathered = lax.all_gather(sigma_top, ('leaf', 'row', 'col'), axis=0)  18.1 us
  transfers between devices with their start and end apart: 9, of which 8 were waited for; matrix products, arithmetic and copies ran while one was open for 15% of the time, Pallas kernels for 0%

commit v1 on v0

--- a/solution.py
+++ b/solution.py
@@ -54,7 +54,7 @@
     positions = slot_count + own_tiles
     band = width // row_count
     partial_factor = mm(panel, inverse)
-    factor_rows = lax.psum(partial_factor, "col")
+    factor_rows = jnp.sum(lax.all_gather(partial_factor, "col"), axis=0)
     living = jnp.concatenate([jnp.ones((1, slot_count), jnp.bool_), picks_all >= 0], axis=0)
     live_here = jnp.take(living, r, axis=1).astype(jnp.float32)
     factor_rows = factor_rows * live_here[:, None, None]

time: 461 us -> 553 us (1.20)
  waiting for transfers between devices: 252 us -> 337 us
  other arithmetic: 53.9 us -> 60.2 us
    all_gather x0 -> x1, waiting for transfers between devices: none -> 75.9 us  [body(): factor_rows = jnp.sum(lax.all_gather(partial_factor, 'col'), axis=0)]
    psum x1 -> x0, waiting for transfers between devices: 57.6 us -> none  [body(): factor_rows = lax.psum(partial_factor, 'col')]
    all_gather x1, waiting for transfers between devices: 18.1 us -> 56.6 us  [body(): gathered = lax.all_gather(sigma_top, ('leaf', 'row', 'col'), axis=0)]
    reduce_scatter x1, waiting for transfers between devices: 0.02 us -> 22.6 us  [body(): lax.psum_scatter(partial_gram, 'col', scatter_dimension=2, tiled=True)]
    unnamed x92 -> x96, local copies, waits for them, and re-layouts: 35.4 us -> 35.4 us
  transfers between devices with their start and end apart: 9 -> 9, of which waited for: 8 -> 9; matrix products, arithmetic and copies ran while one was open for 15% -> 14% of each run, Pallas kernels for 0% -> 0%
where the time goes in v1:
time: 553 us; the launch traced here: 551 us
  waiting for transfers between devices  337 us (61%)
  local copies, waits for them, and re-layouts  104 us (19%)
  other arithmetic  60.2 us (11%)
  between operations  24.9 us (5%)
  matrix products  24.4 us (4%)
    all_gather x1, waiting for transfers between devices, body(): factor_rows = jnp.sum(lax.all_gather(partial_factor, 'col'), axis=0)  75.9 us
    reduce_scatter x2, waiting for transfers between devices, reduce_and_gather(): lax.psum_scatter(diag_partial(first, products), 'row', scatter_dimension=...  63.8 us
    psum x1, waiting for transfers between devices, body(): diag_2 = lax.psum(diag_partial(first_2, product_2) + gram_rows, 'row')  57.9 us
    all_gather x1, waiting for transfers between devices, body(): gathered = lax.all_gather(sigma_top, ('leaf', 'row', 'col'), axis=0)  56.6 us
    unnamed x96, local copies, waits for them, and re-layouts  35.4 us
    all_gather x2, waiting for transfers between devices, reduce_and_gather(): everything = lax.all_gather(both, ('row', 'col'), axis=0)  34.4 us
    all_gather x1, waiting for transfers between devices, body(): factor_cols = lax.all_gather(factor_tile, 'row', axis=1, tiled=True)  25.1 us
    dot_general x12, matrix products, mm(): jnp.matmul(a, b, precision=HIGHEST, preferred_element_type=jnp.float32)  24.4 us
  transfers between devices with their start and end apart: 9, of which 9 were waited for; matrix products, arithmetic and copies ran while one was open for 14% of the time, Pallas kernels for 0%

profile of v1, /device:TPU:0, one launch (start us, length us, event | category | flops | bytes accessed | tf_op | source)
XLA Modules:
  0.0 551.4 jit_solution(5935152266696628289)
XLA Ops:
  8.7 3.9 fusion.2
  13.7 75.9 %all-gather.14.cloned.1.call-done = f32[28,128,512]{2,1,0:T(8,128)} async-done(((f32[7,128,512]{2,1,0:T(8,128)}), f32[28,128,512]{2,1,0:T(8,128)}) %all-gather.14.cloned.1.call-update) | async-done | bytes 7340048 | tf_op jit(solution)/shard_map/all_gather | solution.py:57
  89.6 5.4 reduce_sum.9
  95.0 2.7 copy.91
  97.7 1.7 broadcast_multiply_fusion
  101.5 2.2 fusion
  103.8 56.6 %all-gather.12.cloned.1.call-done = f32[4096,256]{1,0:T(8,128)} async-done(((f32[32,256]{1,0:T(8,128)}), f32[4096,256]{1,0:T(8,128)}) %all-gather.12.cloned.1.call-update) | async-done | bytes 4194320 | tf_op jit(solution)/shard_map/all_gather | solution.py:67
  160.4 5.8 %copy.90 = f32[32,4,32,256]{3,1,2,0:T(4,128)S(1)} copy(f32[32,4,32,256]{3,2,1,0:T(8,128)} %bitcast.196) | data formatting | bytes 8388608 | tf_op jit(solution)/shard_map/reshape | solution.py:68
  166.2 3.0 copy.140
  169.2 25.1 %all-gather.10.cloned.1.call-done = f32[7,1024,128]{1,2,0:T(8,128)} async-done(((f32[7,128,128]{1,2,0:T(8,128)}), f32[7,1024,128]{1,2,0:T(8,128)}) %all-gather.10.cloned.1.call-update) | async-done | bytes 3670032 | tf_op jit(solution)/shard_map/all_gather | solution.py:62
  194.3 2.4 bitcast_dynamic-update-slice_fusion.6
  197.8 22.6 %reduce-scatter.6.cloned.1.call-done = f32[7,64,128]{2,1,0:T(8,128)} async-done(((f32[7,64,512]{2,1,0:T(8,128)}), f32[7,64,128]{2,1,0:T(8,128)}) %reduce-scatter.6.cloned.1.call-update) | async-done | bytes 229392 | tf_op jit(solution)/shard_map/reduce_scatter | solution.py:65
  220.4 33.3 %reduce-scatter.4.cloned.1.call-done = f32[1,64,128]{2,1,0:T(8,128)} async-done(((f32[1,512,128]{2,1,0:T(8,128)}), f32[1,64,128]{2,1,0:T(8,128)}) %reduce-scatter.4.cloned.1.call-update) | async-done | bytes 32784 | tf_op jit(solution)/shard_map/reduce_scatter | solution.py:79
  264.5 2.3 constant_dynamic-slice_fusion.22
  266.8 3.3 fusion.102
  272.6 2.2 select_select_fusion.4
  275.9 24.1 %all-gather.16.cloned.1.call-done = f32[32,192,128]{2,1,0:T(8,128)} async-done(((f32[1,192,128]{2,1,0:T(8,128)}), f32[32,192,128]{2,1,0:T(8,128)}) %all-gather.16.cloned.1.call-update) | async-done | bytes 3145744 | tf_op jit(solution)/shard_map/all_gather | solution.py:84
  301.2 3.2 slice.189
  304.4 2.9 copy.130
  307.3 2.1 copy.149
  314.3 1.8 neg.74
  316.1 1.8 copy.132
  318.9 2.9 bitcast_dynamic-update-slice_fusion.5
  321.8 1.6 bitcast_dynamic-update-slice_fusion.4
  324.8 30.5 %reduce-scatter.8.cloned.1.call-done = f32[2,64,128]{2,1,0:T(8,128)} async-done(((f32[2,512,128]{2,1,0:T(8,128)}), f32[2,64,128]{2,1,0:T(8,128)}) %reduce-scatter.8.cloned.1.call-update) | async-done | bytes 65552 | tf_op jit(solution)/shard_map/reduce_scatter | solution.py:79
  370.7 2.5 gather_fusion.9
  377.7 2.4 select_select_fusion
  383.2 1.9 copy.139
  395.3 10.3 %all-gather.18.cloned.1.call-done = f32[64,192,128]{2,1,0:T(8,128)} async-done(((f32[2,192,128]{2,1,0:T(8,128)}), f32[64,192,128]{2,1,0:T(8,128)}) %all-gather.18.cloned.1.call-update) | async-done | bytes 6291472 | tf_op jit(solution)/shard_map/all_gather | solution.py:84
  405.6 3.2 slice.195
  408.8 4.7 slice.194
  413.5 5.3 copy.134
  418.8 4.9 reshape.293
  423.6 4.3 copy.150
  428.0 3.1 reshape.294
  431.1 4.2 select_bitcast_fusion.4
  439.5 7.9 %select_bitcast_fusion = (f32[1024,512]{0,1:T(8,128)}, f32[1,1024,512]{1,2,0:T(8,128)}, f32[1,1024,512]{1,2,0:T(8,128)}, f32[1,1024,512]{1,2,0:T(8,128)}) fusion(f32[2,1024,512]{1,2,0:T(8,128)} %reshape.293, s32[]{:T(128)S(6)} %select_n.346, pred[]{:T(512)S(6)} %and.78, s32[]{:T(128)S(6)} %select_n.326, s32[]{:T(128)S(6)} %select_n.316, s32[]{:T(128)S(6)} %select_n.336), kind=kLoop, calls=%fused_computation.12 | loop fusion | flops 524288 | bytes 16777232 | tf_op jit(solution)/shard_map/jit(_take)/select_n | solution.py:127
  447.4 2.9 copy.137
  450.3 1.9 select_bitcast_fusion.2
  454.2 1.9 negate_bitcast_fusion
  457.5 3.0 copy.135
  460.4 1.9 select_bitcast_fusion.3
  464.3 2.9 copy.138
  467.2 1.9 select_bitcast_fusion.1
  471.2 3.3 bitcast_dynamic-update-slice_fusion.3
  474.6 1.6 bitcast_dynamic-update-slice_fusion.2
  484.4 57.9 %all-reduce.3.cloned.1.call-done = f32[4,512,128]{2,1,0:T(8,128)} async-done(((f32[4,512,128]{2,1,0:T(8,128)}), f32[4,512,128]{2,1,0:T(8,128)}) %all-reduce.3.cloned.1.call-update) | async-done | bytes 1048592 | tf_op jit(solution)/shard_map/psum | solution.py:157
  542.3 2.6 maximum_bitcast_fusion
  (213 shorter events, 71.2 us)
Async XLA Ops:
  7.2 1.5 copy-start
  7.2 6.2 %copy-start.39 = (s32[1,6,8]{2,0,1:T(1,128)S(1)}, s32[1,6,8]{2,0,1:T(1,128)}, u32[]{:S(2)}) copy-start(s32[1,6,8]{2,0,1:T(1,128)} %param.18) | copy-start | bytes 580
  7.2 82.4 %all-gather.14.cloned.1.call-start = ((), (), s32[]{:S(2)}) async-start(), calls=%async_computation.9 | async-start | bytes 9175040 | tf_op jit(solution)/shard_map/all_gather | solution.py:57
  12.6 147.9 %all-gather.12.cloned.1.call-start = ((), (), s32[]{:S(2)}) async-start(), calls=%async_computation.8 | async-start | bytes 4227072 | tf_op jit(solution)/shard_map/all_gather | solution.py:67
  13.3 181.0 %all-gather.10.cloned.1.call-start = ((), (), s32[]{:S(2)}) async-start(), calls=%async_computation.3 | async-start | bytes 4128768 | tf_op jit(solution)/shard_map/all_gather | solution.py:62
  99.4 1.2 copy-start.2
  101.5 118.9 %reduce-scatter.6.cloned.1.call-start = ((), (), s32[]{:S(2)}) async-start(), calls=%async_computation.5 | async-start | bytes 1146880 | tf_op jit(solution)/shard_map/reduce_scatter | solution.py:65
  103.8 149.9 %reduce-scatter.4.cloned.1.call-start = ((), (), s32[]{:S(2)}) async-start(), calls=%async_computation.4 | async-start | bytes 294912 | tf_op jit(solution)/shard_map/reduce_scatter | solution.py:79
  166.2 30.5 %copy-start.3 = (f32[7,128,512]{1,2,0:T(8,128)S(1)}, f32[7,128,512]{1,2,0:T(8,128)}, u32[]{:S(2)}) copy-start(f32[7,128,512]{1,2,0:T(8,128)} %copy-done.2) | copy-start | bytes 5505028
  197.8 102.1 %all-gather.16.cloned.1.call-start = ((), (), s32[]{:S(2)}) async-start(), calls=%async_computation.10 | async-start | bytes 3244032 | tf_op jit(solution)/shard_map/all_gather | solution.py:84
  255.1 100.2 %reduce-scatter.8.cloned.1.call-start = ((), (), s32[]{:S(2)}) async-start(), calls=%async_computation.6 | async-start | bytes 589824 | tf_op jit(solution)/shard_map/reduce_scatter | solution.py:79
  310.1 2.4 copy-start.5
  314.3 7.5 %copy-start.14 = (f32[12,128,128]{2,1,0:T(8,128)S(1)}, f32[12,128,128]{2,1,0:T(8,128)}, u32[]{:S(2)}) copy-start(f32[12,128,128]{2,1,0:T(8,128)} %select_select_fusion.4) | copy-start | bytes 2359300
  317.9 3.9 copy-start.22
  317.9 3.9 copy-start.32
  323.4 33.8 %copy-start.40 = (s32[1,4]{1,0:T(1,128)S(1)}, s32[1,4]{1,0:T(1,128)}, u32[]{:S(2)}) copy-start(s32[1,4]{1,0:T(1,128)} %param.19) | copy-start | bytes 52
  323.4 44.7 %copy-start.19 = (f32[1,1024,128]{1,2,0:T(8,128)S(1)}, f32[1,1024,128]{1,2,0:T(8,128)}, u32[]{:S(2)}) copy-start(f32[1,1024,128]{1,2,0:T(8,128)} %get-tuple-element.69) | copy-start | bytes 1572868
  323.4 45.7 %copy-start.18 = (f32[1,1024,128]{1,2,0:T(8,128)S(1)}, f32[1,1024,128]{1,2,0:T(8,128)}, u32[]{:S(2)}) copy-start(f32[1,1024,128]{1,2,0:T(8,128)} %get-tuple-element.70) | copy-start | bytes 1572868
  324.7 44.5 %copy-start.17 = (f32[1,1024,128]{1,2,0:T(8,128)S(1)}, f32[1,1024,128]{1,2,0:T(8,128)}, u32[]{:S(2)}) copy-start(f32[1,1024,128]{1,2,0:T(8,128)} %get-tuple-element.71) | copy-start | bytes 1572868
  324.8 80.8 %all-gather.18.cloned.1.call-start = ((), (), s32[]{:S(2)}) async-start(), calls=%async_computation.11 | async-start | bytes 6488064 | tf_op jit(solution)/shard_map/all_gather | solution.py:84
  356.9 185.5 %all-reduce.3.cloned.1.call-start = ((), (), s32[]{:S(2)}) async-start(), calls=%async_computation.7 | async-start | bytes 2097152 | tf_op jit(solution)/shard_map/psum | solution.py:157
  377.7 2.4 copy-start.10
  377.7 3.5 copy-start.9
  377.7 4.5 copy-start.8
  381.1 4.0 copy-start.21
  381.1 5.0 copy-start.20
  383.2 6.2 %copy-start.16 = (f32[1024,128]{0,1:T(8,128)S(1)}, f32[1024,128]{0,1:T(8,128)}, u32[]{:S(2)}) copy-start(f32[1024,128]{0,1:T(8,128)} %get-tuple-element.77) | copy-start | bytes 1572868
  386.3 6.6 %copy-start.15 = (f32[1024,128]{0,1:T(8,128)S(1)}, f32[1024,128]{0,1:T(8,128)}, u32[]{:S(2)}) copy-start(f32[1024,128]{0,1:T(8,128)} %get-tuple-element.78) | copy-start | bytes 1572868
  389.7 4.9 copy-start.24
  450.3 2.7 copy-start.36
  453.0 4.1 copy-start.33
  460.4 2.7 copy-start.35
  467.2 2.7 copy-start.34
  471.1 3.4 copy-start.6
  471.1 3.4 copy-start.13
  471.1 3.4 copy-start.26
  471.1 3.4 copy-start.28
  471.1 3.4 copy-start.31
  471.2 5.0 copy-start.7
  471.2 5.0 copy-start.12
  471.2 5.0 copy-start.25
  471.2 5.0 copy-start.29
  471.2 5.0 copy-start.30
  474.6 3.2 copy-start.11
  474.6 3.2 copy-start.23
  474.6 3.2 copy-start.27
  480.4 2.0 copy-start.37
  483.2 61.7 %copy-start.1 = (f32[1,7,128,512]{3,2,1,0:T(8,128)S(1)}, f32[1,7,128,512]{3,2,1,0:T(8,128)}, u32[]{:S(2)}) copy-start(f32[1,7,128,512]{3,2,1,0:T(8,128)} %param.17) | copy-start | bytes 5505028
  (2 other events, 2.0 us)
Sparse Core Ops, SparseCore 0:
  12.7 76.8 all-gather.13
  92.7 67.6 all-gather.11
  162.7 31.5 all-gather.9
  196.6 23.7 reduce-scatter.5
  223.2 30.4 reduce-scatter.3
  256.0 43.8 all-gather.15
  324.9 30.3 reduce-scatter.7
  357.5 48.0 all-gather.17
  481.5 60.7 all-reduce.2
